TPU v7x, 128 devices: a whole 4x4x4 slice. The times are simulated.
128 devices in a mesh: dp: 4 (over x), tensor: 32 (over y, z, core).
Axes of the slice: x: 4, y: 4, z: 4, core: 2. Of those that a mesh axis runs over, the one named last changes fastest.
Arguments:
- tokens: bfloat16 [16384, 2048], P(('dp', 'tensor')), may hold values from -6 to 6
- norm_gain: bfloat16 [2048], replicated, may hold values from 0.099609375 to 1.8984375
- routes: int32 [16384, 6], P(('dp', 'tensor')), may hold values from 0 to 31, all different within a row; in each aligned block of 128 rows (0 to 127, 128 to 255, ...) at most 32 rows name the same one
- route_gates: bfloat16 [16384, 6], P(('dp', 'tensor')), may hold values from 0.19921875 to 1
- lengths: int32 [24], replicated, may hold values from 1 to 1920, 16384 in all
- request_adapter: int32 [24], replicated, may hold values from 0 to 31
- adapter_slot: int32 [32], replicated, may hold values from 0 to 31, each once
- expert_gate: bfloat16 [32, 2048, 1408], P('tensor'), may hold values from -0.125 to 0.125
- expert_up: bfloat16 [32, 2048, 1408], P('tensor'), may hold values from -0.125 to 0.125
- expert_down: bfloat16 [32, 1408, 2048], P('tensor'), may hold values from -0.15625 to 0.15625
- shared_gate: bfloat16 [2048, 1408], P(None, 'dp'), may hold values from -0.125 to 0.125
- shared_up_weight: bfloat16 [2048, 1408], P(None, 'dp'), may hold values from -0.125 to 0.125
- shared_down: bfloat16 [1408, 2048], P('dp'), may hold values from -0.15625 to 0.15625
- adapter_down: bfloat16 [32, 2048, 16], P('dp'), may hold values from -0.125 to 0.125
- adapter_up: bfloat16 [32, 16, 2048], P('dp'), may hold values from -1.5 to 1.5
- head_weight: bfloat16 [2048, 65536], P(None, ('dp', 'tensor')), may hold values from -0.375 to 0.375
Outputs:
- sublayer_out: bfloat16 [16384, 2048], P(('dp', 'tensor'))
- last_norm: float32 [24], replicated
- block_logit: float32 [24, 32], P(None, 'tensor')
Inputs may be any that keep to these rules, and one draw needn't show every extreme that they name: `routes`: in each aligned block of 128 rows (the rows of one device), no expert is named by more than 32 rows, a bound that some block reaches. The lengths sum to 16384; the largest is exactly 1920. Each position of the store appears once: adapter a is stored at position adapter_slot[a] of adapter_down and adapter_up.
All inputs are finite; a program needn't handle non-finite values.
Results may differ from a plain program's by a relative error of at most 0.0066.
Values may be sent and summed in bfloat16 or wider, within the bound.
A program may use at most 128 MiB of HBM per device.

v0:
```python
import jax
import jax.numpy as jnp
from jax import lax
from jax.sharding import PartitionSpec as P

CAP = 32


def apply_norm(tokens, norm_gain):
    values = tokens.astype(jnp.float32)
    scaled = lax.rsqrt(jnp.mean(values * values, axis=-1, keepdims=True) + 1e-06)
    return (values * scaled * norm_gain.astype(jnp.float32)).astype(jnp.bfloat16)


def feed_forward(inputs, gate_mat, up_mat, down_mat):
    gate_portion = jnp.dot(inputs, gate_mat, preferred_element_type=jnp.float32)
    up_part = jnp.dot(inputs, up_mat, preferred_element_type=jnp.float32)
    hidden = (jax.nn.silu(gate_portion) * up_part).astype(jnp.bfloat16)
    return jnp.dot(hidden, down_mat, preferred_element_type=jnp.float32)


def token_slots(positions, lengths, request_adapter, adapter_slot):
    request_ends = jnp.cumsum(lengths)
    request = jnp.sum((request_ends[None, :] <= positions[:, None]).astype(jnp.int32), axis=1)
    request_pick = (
        request[:, None] == jnp.arange(request_adapter.shape[0], dtype=jnp.int32)[None, :]
    )
    adapter = jnp.sum(jnp.where(request_pick, request_adapter[None, :], 0), axis=1)
    adapter_pick = adapter[:, None] == jnp.arange(adapter_slot.shape[0], dtype=jnp.int32)[None, :]
    return jnp.sum(jnp.where(adapter_pick, adapter_slot[None, :], 0), axis=1)


def adapter_delta(inputs, slot_ids, down_store, up_store):
    held_count = down_store.shape[0]
    model_width = down_store.shape[1]
    rank_size = down_store.shape[2]
    flat_down = jnp.transpose(down_store, (1, 0, 2)).reshape(model_width, held_count * rank_size)
    low_rank = jnp.dot(inputs, flat_down, preferred_element_type=jnp.float32)
    low_rank = low_rank.reshape(inputs.shape[0], held_count, rank_size)
    keep_mask = slot_ids[:, None] == jnp.arange(held_count, dtype=jnp.int32)[None, :]
    low_rank = jnp.where(keep_mask[:, :, None], low_rank, 0.0).astype(jnp.bfloat16)
    low_rank = low_rank.reshape(inputs.shape[0], held_count * rank_size)
    flat_up = up_store.reshape(held_count * rank_size, up_store.shape[2])
    return jnp.dot(low_rank, flat_up, preferred_element_type=jnp.float32)


def local(
    tokens,
    norm_gain,
    routes,
    route_gates,
    lengths,
    request_adapter,
    adapter_slot,
    expert_gate,
    expert_up,
    expert_down,
    shared_gate,
    shared_up_weight,
    shared_down,
    adapter_down,
    adapter_up,
    head_weight,
):
    tok_rows = tokens.shape[0]
    model_width = tokens.shape[1]
    route_count = routes.shape[1]
    tensor_size = lax.axis_size("tensor")
    tensor_pos = lax.axis_index("tensor")
    data_pos = lax.axis_index("dp")
    local_experts = expert_gate.shape[0]
    all_experts = local_experts * tensor_size
    slot_range = jnp.arange(CAP, dtype=jnp.int32)
    normed = apply_norm(tokens, norm_gain)
    numbers = jnp.arange(all_experts, dtype=jnp.int32)
    route_hits = routes[:, :, None] == numbers[None, None, :]
    chosen = jnp.any(route_hits, axis=1)
    weight = jnp.sum(
        jnp.where(route_hits, route_gates[:, :, None], jnp.zeros((), jnp.bfloat16)), axis=1
    )
    slot_place = jnp.cumsum(chosen.astype(jnp.int32), axis=0) - 1
    pooled, pooled_routes = (
        lax.all_gather(normed, "tensor", axis=0, tiled=True),
        lax.all_gather(routes.astype(jnp.bfloat16), "tensor", axis=0, tiled=True),
    )
    pooled = pooled.reshape(tensor_size, tok_rows, model_width)
    source_routes = pooled_routes.astype(jnp.int32).reshape(tensor_size, tok_rows, route_count)
    own_numbers = tensor_pos * local_experts + jnp.arange(local_experts, dtype=jnp.int32)
    source_hits = source_routes[:, :, :, None] == own_numbers[None, None, None, :]
    source_chosen = jnp.any(source_hits, axis=2)
    source_place = jnp.cumsum(source_chosen.astype(jnp.int32), axis=1) - 1
    source_pick = source_chosen[:, :, :, None] & (
        source_place[:, :, :, None] == slot_range[None, None, None, :]
    )
    source_pick = jnp.where(source_pick, 1.0, 0.0).astype(jnp.bfloat16)
    incoming = jnp.einsum(
        "sijc,sid->sjcd", source_pick, pooled, preferred_element_type=jnp.float32
    ).astype(jnp.bfloat16)
    gate_portion = jnp.einsum(
        "secd,edf->secf", incoming, expert_gate, preferred_element_type=jnp.float32
    )
    up_part = jnp.einsum("secd,edf->secf", incoming, expert_up, preferred_element_type=jnp.float32)
    hidden = (jax.nn.silu(gate_portion) * up_part).astype(jnp.bfloat16)
    expert_out = jnp.einsum(
        "secf,efd->secd", hidden, expert_down, preferred_element_type=jnp.float32
    ).astype(jnp.bfloat16)
    returned_rows = lax.all_to_all(expert_out, "tensor", split_axis=0, concat_axis=0, tiled=True)
    returned_rows = returned_rows.reshape(all_experts, CAP, model_width)
    mixing_result = jnp.where(
        slot_place[:, :, None] == slot_range[None, None, :],
        weight[:, :, None],
        jnp.zeros((), jnp.bfloat16),
    )
    routed_output = jnp.einsum(
        "kbt,btw->kw", mixing_result, returned_rows, preferred_element_type=jnp.float32
    )
    own_base = (data_pos * tensor_size + tensor_pos) * tok_rows
    own_positions = own_base + jnp.arange(tok_rows, dtype=jnp.int32)
    peer_rows = lax.all_gather(normed, "dp", axis=0, tiled=True)
    shared_sum = lax.psum_scatter(
        feed_forward(peer_rows, shared_gate, shared_up_weight, shared_down),
        "dp",
        scatter_dimension=0,
        tiled=True,
    )
    own_slots = token_slots(own_positions, lengths, request_adapter, adapter_slot)
    store_down, store_up = (
        lax.all_gather(adapter_down, "dp", axis=0, tiled=True),
        lax.all_gather(adapter_up, "dp", axis=0, tiled=True),
    )
    summed = routed_output + shared_sum + adapter_delta(normed, own_slots, store_down, store_up)
    sublayer_out = summed.astype(jnp.bfloat16)
    request_ends = jnp.cumsum(lengths)
    last_pick = jnp.where(request_ends[:, None] - 1 == own_positions[None, :], 1.0, 0.0).astype(
        jnp.bfloat16
    )
    last_part = jnp.dot(last_pick, sublayer_out, preferred_element_type=jnp.float32)
    last_states = lax.psum(last_part, ("dp", "tensor"))
    last_norm = jnp.sqrt(jnp.sum(last_states * last_states, axis=1))
    logits = jnp.dot(
        last_states.astype(jnp.bfloat16), head_weight, preferred_element_type=jnp.float32
    )
    block_logit = lax.pmax(jnp.max(logits, axis=1), "dp")
    return (sublayer_out, last_norm, block_logit[:, None])


def solution(mesh):
    placed = (
        P(("dp", "tensor"), None),
        P(),
        P(("dp", "tensor"), None),
        P(("dp", "tensor"), None),
        P(),
        P(),
        P(),
        P("tensor", None, None),
        P("tensor", None, None),
        P("tensor", None, None),
        P(None, "dp"),
        P(None, "dp"),
        P("dp", None),
        P("dp", None, None),
        P("dp", None, None),
        P(None, ("dp", "tensor")),
    )
    return jax.shard_map(
        local,
        mesh=mesh,
        in_specs=placed,
        out_specs=(P(("dp", "tensor"), None), P(), P(None, "tensor")),
        check_vma=False,
    )
```

profile of v0, /device:TPU:0, one launch (start us, length us, event | category | flops | bytes accessed | tf_op | source)
XLA Modules:
  0.0 401.9 jit_solution(9235097486257809376)
XLA Ops:
  7.2 0.0 copy-start
  7.2 0.0 copy-start.8
  7.2 0.0 all-gather.7.cloned.1.call-start
  7.2 0.9 convert_element_type.84
  8.1 1.3 fusion.41
  9.4 2.0 fusion.43
  11.4 0.0 all-gather.7.cloned.1.call-update
  11.5 0.0 all-gather.5.cloned.1.call-start
  11.5 0.7 all-gather.5.cloned.1.call-update
  12.2 0.0 reduce-scatter.2.cloned.1.call-start
  12.3 32.6 %all-gather.7.cloned.1.call-done = bf16[512,2048]{1,0:T(8,128)(2,1)} async-done(((bf16[128,2048]{1,0:T(8,128)(2,1)}), bf16[512,2048]{1,0:T(8,128)(2,1)}) %all-gather.7.cloned.1.call-update) | async-done | bytes 2097168 | tf_op jit(solution)/shard_map/all_gather | solution.py:119
  44.9 3.8 fusion.82
  48.7 0.0 copy-done.8
  48.7 6.3 %fusion.32 = f32[512,2048]{1,0:T(8,128)} fusion(bf16[352,2048]{1,0:T(8,128)(2,1)S(1)} %copy-done.8, bf16[512,2048]{1,0:T(8,128)(2,1)} %all-gather.7.cloned.1.call-done, bf16[2048,352]{0,1:T(8,128)(2,1)} %param.27, f32[512,352]{0,1:T(8,128)} %fusion.82), kind=kOutput, calls=%fused_computation.29 | convolution fusion | flops 1477476352 | bytes 9895936 | tf_op jit(solution)/shard_map/dot_general | solution.py:19
  55.0 0.0 reduce-scatter.2.cloned.1.call-update
  55.0 0.0 all-gather.11.cloned.1.call-start
  55.1 1.0 copy-done.4
  56.0 1.1 copy.47
  57.1 0.0 all-gather.11.cloned.1.call-update
  57.1 0.0 copy-done.5
  57.2 24.6 %all_gather.15 = bf16[4096,6]{0,1:T(8,128)(2,1)S(1)} all-gather(bf16[128,6]{0,1:T(8,128)(2,1)S(1)} %convert_element_type.79), channel_id=1, replica_groups=mesh['dp'=4,'tensor'=32] {'tensor'}, dimensions={0}, use_global_device_ids=true | all-gather | bytes 50688 | tf_op jit(solution)/shard_map/all_gather | solution.py:84
  81.7 0.1 fusion.63
  81.8 0.3 reduce_window_sum.31
  82.1 38.3 %all-gather.5.cloned.1.call-done = bf16[4096,2048]{1,0:T(8,128)(2,1)} async-done(((bf16[128,2048]{1,0:T(8,128)(2,1)}), bf16[4096,2048]{1,0:T(8,128)(2,1)}) %all-gather.5.cloned.1.call-update) | async-done | bytes 16777232 | tf_op jit(solution)/shard_map/all_gather | solution.py:83
  120.4 8.1 %convolution_convert_fusion = bf16[32,32,2048]{2,1,0:T(8,128)(2,1)S(1)} fusion(bf16[32,128,2048]{2,1,0:T(8,128)(2,1)} %bitcast.109, s32[32,128]{1,0:T(8,128)S(1)} %broadcast_add_fusion.1, pred[32,128]{1,0:T(8,128)(4,1)S(1)} %bitcast.111), kind=kOutput, calls=%fused_computation.16 | convolution fusion | flops 539492352 | bytes 20992000 | tf_op jit(solution)/shard_map/sijc,sid->sjcd/dot_general | solution.py:96
  128.5 0.0 copy-start.1
  128.5 2.1 copy-done.1
  130.6 10.7 %fusion.3 = f32[32,32,1408]{2,1,0:T(8,128)} fusion(bf16[32,32,2048]{2,1,0:T(8,128)(2,1)S(1)} %convolution_convert_fusion, bf16[1,2048,1408]{2,1,0:T(8,128)(2,1)} %param.24), kind=kOutput, calls=%fused_computation.4 | convolution fusion | flops 5905580032 | bytes 15728640 | tf_op jit(solution)/shard_map/secd,edf->secf/dot_general | solution.py:102
  141.3 21.0 %convert_bitcast_fusion = bf16[32,1,32,2048]{3,2,1,0:T(8,128)(2,1)} fusion(bf16[1,1408,2048]{2,1,0:T(8,128)(2,1)} %param.25, f32[32,32,1408]{2,1,0:T(8,128)} %fusion.3, bf16[32,32,2048]{2,1,0:T(8,128)(2,1)} %copy-done.1, bf16[1,2048,1408]{2,1,0:T(8,128)(2,1)} %param.23), kind=kOutput, calls=%fused_computation.15 | convolution fusion | flops 11821907968 | bytes 25690112 | tf_op jit(solution)/shard_map/secf,efd->secd/dot_general | solution.py:104
  162.4 0.0 copy-start.6
  162.4 5.2 %all-to-all-start = ((bf16[32,1,32,2048]{3,2,1,0:T(8,128)(2,1)}), bf16[32,1,32,2048]{3,2,1,0:T(8,128)(2,1)}, u32[]{:S(2)}, u32[]{:S(2)}) async-start(bf16[32,1,32,2048]{3,2,1,0:T(8,128)(2,1)} %convert_bitcast_fusion), calls=%async_computation | async-start | bytes 8388608 | tf_op jit(solution)/shard_map/all_to_all | solution.py:107
  167.6 0.0 copy-start.2
  167.6 0.0 all-gather.9.cloned.1.call-start
  167.7 0.5 all-gather.9.cloned.1.call-update
  168.2 0.3 all-reduce.2.cloned.1.call-start
  168.5 0.1 copy.42
  168.6 0.2 reduce_window_sum.30
  168.8 0.1 copy.43
  168.8 0.0 copy-done.7
  168.8 0.1 copy.45
  168.9 0.1 reduce-window.7
  169.0 0.1 reduce.2
  169.1 0.1 convert_reduce_fusion
  169.2 0.0 copy-done.9
  169.2 0.1 select_reduce_fusion.1
  169.3 0.0 copy-done.10
  169.3 0.1 select_reduce_fusion
  169.4 0.0 copy-done.6
  169.5 0.0 reduce-scatter.2.cloned.1.call-done
  169.5 50.9 %all-to-all-done = bf16[32,1,32,2048]{3,2,1,0:T(8,128)(2,1)} async-done(((bf16[32,1,32,2048]{3,2,1,0:T(8,128)(2,1)}), bf16[32,1,32,2048]{3,2,1,0:T(8,128)(2,1)}, u32[]{:S(2)}, u32[]{:S(2)}) %all-to-all-start) | async-done | bytes 4194336 | tf_op jit(solution)/shard_map/all_to_all | solution.py:107
  220.4 4.3 %fusion.23 = f32[128,2048]{1,0:T(8,128)} fusion(f32[128,2048]{1,0:T(8,128)} %reduce-scatter.2.cloned.1.call-done, bf16[32,1,32,2048]{3,2,1,0:T(8,128)(2,1)} %all-to-all-done, s32[128,32]{0,1:T(8,128)S(1)} %copy.43, bf16[128,32]{0,1:T(8,128)(2,1)S(1)} %fusion.68), kind=kOutput, calls=%fused_computation.21 | convolution fusion | flops 537395200 | bytes 6316032 | tf_op jit(solution)/shard_map/kbt,btw->kw/dot_general | solution.py:114
  224.7 9.1 %all-gather.9.cloned.1.call-done = bf16[32,2048,16]{1,2,0:T(8,128)(2,1)} async-done(((bf16[8,2048,16]{1,2,0:T(8,128)(2,1)}), bf16[32,2048,16]{1,2,0:T(8,128)(2,1)}) %all-gather.9.cloned.1.call-update) | async-done | bytes 2097168 | tf_op jit(solution)/shard_map/all_gather | solution.py:128
  233.7 0.0 copy-done.2
  233.7 4.5 %fusion.26 = bf16[128,2048]{1,0:T(8,128)(2,1)S(1)} fusion(f32[128,2048]{1,0:T(8,128)} %fusion.23, bf16[32,16,2048]{2,0,1:T(8,128)(2,1)} %all-gather.11.cloned.1.call-done, bf16[32,16,2048]{2,1,0:T(8,128)(2,1)} %bitcast.110, bf16[128,2048]{1,0:T(8,128)(2,1)S(1)} %copy-done.2, pred[128,32]{0,1:T(8,128)(4,1)S(1)} %iota_compare_fusion.3), kind=kOutput, calls=%fused_computation.22 | convolution fusion | flops 537526272 | bytes 6295552 | tf_op jit(solution)/shard_map/dot_general | solution.py:44
  238.3 0.0 copy-start.3
  238.3 0.9 fusion.69
  239.2 0.0 all-reduce.2.cloned.1.call-update
  239.2 143.1 %all-reduce.2.cloned.1.call-done = f32[24,2048]{1,0:T(8,128)} async-done(((f32[24,2048]{1,0:T(8,128)}), f32[24,2048]{1,0:T(8,128)}) %all-reduce.2.cloned.1.call-update) | async-done | bytes 196624 | tf_op jit(solution)/shard_map/psum | solution.py:138
  382.3 0.0 copy-done
  382.3 1.4 convolution_reduce_fusion
  383.7 9.7 %pmax.7 = f32[24,1]{0,1:T(1,128)} all-reduce(f32[24,1]{0,1:T(1,128)S(1)} %bitcast.112), channel_id=1, replica_groups=mesh['dp'=4,'tensor'=32] {'dp'}, use_global_device_ids=true, to_apply=%region_14.15 | all-reduce | flops 24 | bytes 192 | tf_op jit(solution)/shard_map/pmax | solution.py:143
  393.5 1.1 multiply_reduce_fusion
  394.6 0.5 sqrt.3
  395.1 0.0 copy-done.3
  (17 shorter events, 0.1 us)
Async XLA Ops:
  7.2 375.2 %copy-start = (bf16[2048,512]{1,0:T(8,128)(2,1)S(1)}, bf16[2048,512]{1,0:T(8,128)(2,1)}, u32[]{:S(2)}) copy-start(bf16[2048,512]{1,0:T(8,128)(2,1)} %param.31) | copy-start | bytes 6291460
  7.2 41.5 %copy-start.8 = (bf16[352,2048]{1,0:T(8,128)(2,1)S(1)}, bf16[352,2048]{1,0:T(8,128)(2,1)}, u32[]{:S(2)}) copy-start(bf16[352,2048]{1,0:T(8,128)(2,1)} %param.28) | copy-start | bytes 4325380
  7.2 37.7 %all-gather.7.cloned.1.call-start = ((), (), s32[]{:S(2)}) async-start(), calls=%async_computation.3 | async-start | bytes 2621440 | tf_op jit(solution)/shard_map/all_gather | solution.py:119
  11.5 109.0 %all-gather.5.cloned.1.call-start = ((), (), s32[]{:S(2)}) async-start(), calls=%async_computation.2 | async-start | bytes 17301504 | tf_op jit(solution)/shard_map/all_gather | solution.py:83
  12.2 157.3 %reduce-scatter.2.cloned.1.call-start = ((), (), s32[]{:S(2)}) async-start(), calls=%async_computation.4 | async-start | bytes 5242880 | tf_op jit(solution)/shard_map/reduce_scatter | solution.py:120
  55.0 1.0 copy-start.4
  55.0 2.1 copy-start.5
  55.0 169.6 %all-gather.11.cloned.1.call-start = ((), (), s32[]{:S(2)}) async-start(), calls=%async_computation.6 | async-start | bytes 2621440 | tf_op jit(solution)/shard_map/all_gather | solution.py:129
  128.5 2.1 copy-start.1
  162.3 6.5 %copy-start.7 = (s32[24]{0:T(128)S(1)}, s32[24]{0:T(128)}, u32[]{:S(2)}) copy-start(s32[24]{0:T(128)} %param.20) | copy-start | bytes 292
  162.3 6.9 %copy-start.9 = (s32[24]{0:T(128)S(1)}, s32[24]{0:T(128)}, u32[]{:S(2)}) copy-start(s32[24]{0:T(128)} %param.21) | copy-start | bytes 292
  162.3 7.0 %copy-start.10 = (s32[32]{0:T(128)S(1)}, s32[32]{0:T(128)}, u32[]{:S(2)}) copy-start(s32[32]{0:T(128)} %param.22) | copy-start | bytes 388
  162.4 7.1 %copy-start.6 = (bf16[128,6]{0,1:T(8,128)(2,1)S(1)}, bf16[128,6]{0,1:T(8,128)(2,1)}, u32[]{:S(2)}) copy-start(bf16[128,6]{0,1:T(8,128)(2,1)} %param.19) | copy-start | bytes 4612
  162.4 58.0 %all-to-all-start = ((bf16[32,1,32,2048]{3,2,1,0:T(8,128)(2,1)}), bf16[32,1,32,2048]{3,2,1,0:T(8,128)(2,1)}, u32[]{:S(2)}, u32[]{:S(2)}) async-start(bf16[32,1,32,2048]{3,2,1,0:T(8,128)(2,1)} %convert_bitcast_fusion), calls=%async_computation | async-start | bytes 8388608 | tf_op jit(solution)/shard_map/all_to_all | solution.py:107
  167.6 66.1 %copy-start.2 = (bf16[128,2048]{1,0:T(8,128)(2,1)S(1)}, bf16[128,2048]{1,0:T(8,128)(2,1)}, u32[]{:S(2)}) copy-start(bf16[128,2048]{1,0:T(8,128)(2,1)} %fusion.43) | copy-start | bytes 1572868
  167.6 66.1 %all-gather.9.cloned.1.call-start = ((), (), s32[]{:S(2)}) async-start(), calls=%async_computation.5 | async-start | bytes 2621440 | tf_op jit(solution)/shard_map/all_gather | solution.py:128
  168.2 214.1 %all-reduce.2.cloned.1.call-start = ((), (), s32[]{:S(2)}) async-start(), calls=%async_computation.7 | async-start | bytes 393216 | tf_op jit(solution)/shard_map/psum | solution.py:138
  238.3 156.8 %copy-start.3 = (bf16[128,2048]{1,0:T(8,128)(2,1)}, bf16[128,2048]{1,0:T(8,128)(2,1)S(1)}, u32[]{:S(2)}) copy-start(bf16[128,2048]{1,0:T(8,128)(2,1)S(1)} %fusion.26) | copy-start | bytes 1572868
Sparse Core Ops, SparseCore 0:
  11.6 33.2 all-gather.6
  47.7 72.6 all-gather.4
  122.8 46.1 reduce-scatter.1
  170.7 30.5 all-gather.10
  202.9 30.8 all-gather.8
  239.3 142.9 all-reduce.1
where the time goes:
time: 402 us
  waiting for transfers between devices  275 us (68%)
  matrix products  61.1 us (15%)
  blocking collectives  34.3 us (9%)
  between operations  14.3 us (4%)
  other arithmetic  6.28 us (2%)
  starting transfers between devices  5.69 us (1%)
  local copies, waits for them, and re-layouts  4.94 us (1%)
    psum x1, waiting for transfers between devices, local(): last_states = lax.psum(last_part, ('dp', 'tensor'))  143 us
    all_to_all x1, waiting for transfers between devices, local(): lax.all_to_all(expert_out, 'tensor', split_axis=0, concat_axis=0, tiled=T...  50.9 us
    all_gather x1, waiting for transfers between devices, local(): lax.all_gather(normed, 'tensor', axis=0, tiled=True)  38.3 us
    all_gather x1, waiting for transfers between devices, local(): peer_rows = lax.all_gather(normed, 'dp', axis=0, tiled=True)  32.6 us
    all_gather x1, blocking collectives, local(): lax.all_gather(routes.astype(jnp.bfloat16), 'tensor', axis=0, tiled=True)  24.6 us
    dot_general x1, matrix products, local(): jnp.einsum('secf,efd->secd', hidden, expert_down, preferred_element_type=...  21 us
    dot_general x1, matrix products, local(): jnp.einsum('secd,edf->secf', incoming, expert_up, preferred_element_type=...  10.7 us
    pmax x1, blocking collectives, local(): block_logit = lax.pmax(jnp.max(logits, axis=1), 'dp')  9.75 us
  transfers between devices with their start and end apart: 7, of which 5 were waited for; matrix products, arithmetic and copies ran while one was open for 14% of the time, Pallas kernels for 0%

commit v1 on v0

--- a/solution.py
+++ b/solution.py
@@ -135,7 +135,7 @@
         jnp.bfloat16
     )
     last_part = jnp.dot(last_pick, sublayer_out, preferred_element_type=jnp.float32)
-    last_states = lax.psum(last_part, ("dp", "tensor"))
+    last_states = lax.psum(lax.psum(last_part, "tensor"), "dp")
     last_norm = jnp.sqrt(jnp.sum(last_states * last_states, axis=1))
     logits = jnp.dot(
         last_states.astype(jnp.bfloat16), head_weight, preferred_element_type=jnp.float32

time: 402 us -> 402 us (level)
    psum x1 -> x2, waiting for transfers between devices: 143 us -> 142 us  [local(): last_states = lax.psum(lax.psum(last_part, 'tensor'), 'dp')]
  transfers between devices with their start and end apart: 7 -> 8, of which waited for: 5 -> 6; matrix products, arithmetic and copies ran while one was open for 14% -> 14% of each run, Pallas kernels for 0% -> 0%
where the time goes in v1:
time: 402 us; the launch traced here: 401 us
  waiting for transfers between devices  275 us (68%)
  matrix products  61.1 us (15%)
  blocking collectives  34.4 us (9%)
  between operations  14.3 us (4%)
  other arithmetic  6.28 us (2%)
  starting transfers between devices  5.73 us (1%)
  local copies, waits for them, and re-layouts  4.94 us (1%)
    psum x2, waiting for transfers between devices, local(): last_states = lax.psum(lax.psum(last_part, 'tensor'), 'dp')  142 us
    all_to_all x1, waiting for transfers between devices, local(): lax.all_to_all(expert_out, 'tensor', split_axis=0, concat_axis=0, tiled=T...  50.9 us
    all_gather x1, waiting for transfers between devices, local(): lax.all_gather(normed, 'tensor', axis=0, tiled=True)  38.3 us
    all_gather x1, waiting for transfers between devices, local(): peer_rows = lax.all_gather(normed, 'dp', axis=0, tiled=True)  32.6 us
    all_gather x1, blocking collectives, local(): lax.all_gather(routes.astype(jnp.bfloat16), 'tensor', axis=0, tiled=True)  24.6 us
    dot_general x1, matrix products, local(): jnp.einsum('secf,efd->secd', hidden, expert_down, preferred_element_type=...  21 us
    dot_general x1, matrix products, local(): jnp.einsum('secd,edf->secf', incoming, expert_up, preferred_element_type=...  10.7 us
    pmax x1, blocking collectives, local(): block_logit = lax.pmax(jnp.max(logits, axis=1), 'dp')  9.85 us
  transfers between devices with their start and end apart: 8, of which 6 were waited for; matrix products, arithmetic and copies ran while one was open for 14% of the time, Pallas kernels for 0%

profile of v1, /device:TPU:0, one launch (start us, length us, event | category | flops | bytes accessed | tf_op | source)
XLA Modules:
  0.0 401.4 jit_solution(15870367274909506602)
XLA Ops:
  7.2 0.0 copy-start
  7.2 0.0 copy-start.8
  7.2 0.0 all-gather.7.cloned.1.call-start
  7.2 0.9 convert_element_type.84
  8.1 1.3 fusion.41
  9.4 2.0 fusion.43
  11.4 0.0 all-gather.7.cloned.1.call-update
  11.5 0.0 all-gather.5.cloned.1.call-start
  11.5 0.7 all-gather.5.cloned.1.call-update
  12.2 0.0 reduce-scatter.2.cloned.1.call-start
  12.3 32.6 %all-gather.7.cloned.1.call-done = bf16[512,2048]{1,0:T(8,128)(2,1)} async-done(((bf16[128,2048]{1,0:T(8,128)(2,1)}), bf16[512,2048]{1,0:T(8,128)(2,1)}) %all-gather.7.cloned.1.call-update) | async-done | bytes 2097168 | tf_op jit(solution)/shard_map/all_gather | solution.py:119
  44.9 3.8 fusion.82
  48.7 0.0 copy-done.8
  48.7 6.3 %fusion.32 = f32[512,2048]{1,0:T(8,128)} fusion(bf16[352,2048]{1,0:T(8,128)(2,1)S(1)} %copy-done.8, bf16[512,2048]{1,0:T(8,128)(2,1)} %all-gather.7.cloned.1.call-done, bf16[2048,352]{0,1:T(8,128)(2,1)} %param.27, f32[512,352]{0,1:T(8,128)} %fusion.82), kind=kOutput, calls=%fused_computation.29 | convolution fusion | flops 1477476352 | bytes 9895936 | tf_op jit(solution)/shard_map/dot_general | solution.py:19
  55.0 0.0 reduce-scatter.2.cloned.1.call-update
  55.0 0.0 all-gather.11.cloned.1.call-start
  55.1 1.0 copy-done.4
  56.0 1.1 copy.47
  57.1 0.0 all-gather.11.cloned.1.call-update
  57.1 0.0 copy-done.5
  57.2 24.6 %all_gather.15 = bf16[4096,6]{0,1:T(8,128)(2,1)S(1)} all-gather(bf16[128,6]{0,1:T(8,128)(2,1)S(1)} %convert_element_type.79), channel_id=1, replica_groups=mesh['dp'=4,'tensor'=32] {'tensor'}, dimensions={0}, use_global_device_ids=true | all-gather | bytes 50688 | tf_op jit(solution)/shard_map/all_gather | solution.py:84
  81.7 0.1 fusion.63
  81.8 0.3 reduce_window_sum.31
  82.1 38.3 %all-gather.5.cloned.1.call-done = bf16[4096,2048]{1,0:T(8,128)(2,1)} async-done(((bf16[128,2048]{1,0:T(8,128)(2,1)}), bf16[4096,2048]{1,0:T(8,128)(2,1)}) %all-gather.5.cloned.1.call-update) | async-done | bytes 16777232 | tf_op jit(solution)/shard_map/all_gather | solution.py:83
  120.4 8.1 %convolution_convert_fusion = bf16[32,32,2048]{2,1,0:T(8,128)(2,1)S(1)} fusion(bf16[32,128,2048]{2,1,0:T(8,128)(2,1)} %bitcast.109, s32[32,128]{1,0:T(8,128)S(1)} %broadcast_add_fusion.1, pred[32,128]{1,0:T(8,128)(4,1)S(1)} %bitcast.111), kind=kOutput, calls=%fused_computation.16 | convolution fusion | flops 539492352 | bytes 20992000 | tf_op jit(solution)/shard_map/sijc,sid->sjcd/dot_general | solution.py:96
  128.5 0.0 copy-start.1
  128.5 2.1 copy-done.1
  130.6 10.7 %fusion.3 = f32[32,32,1408]{2,1,0:T(8,128)} fusion(bf16[32,32,2048]{2,1,0:T(8,128)(2,1)S(1)} %convolution_convert_fusion, bf16[1,2048,1408]{2,1,0:T(8,128)(2,1)} %param.24), kind=kOutput, calls=%fused_computation.4 | convolution fusion | flops 5905580032 | bytes 15728640 | tf_op jit(solution)/shard_map/secd,edf->secf/dot_general | solution.py:102
  141.3 21.0 %convert_bitcast_fusion = bf16[32,1,32,2048]{3,2,1,0:T(8,128)(2,1)} fusion(bf16[1,1408,2048]{2,1,0:T(8,128)(2,1)} %param.25, f32[32,32,1408]{2,1,0:T(8,128)} %fusion.3, bf16[32,32,2048]{2,1,0:T(8,128)(2,1)} %copy-done.1, bf16[1,2048,1408]{2,1,0:T(8,128)(2,1)} %param.23), kind=kOutput, calls=%fused_computation.15 | convolution fusion | flops 11821907968 | bytes 25690112 | tf_op jit(solution)/shard_map/secf,efd->secd/dot_general | solution.py:104
  162.4 0.0 copy-start.6
  162.4 5.2 %all-to-all-start = ((bf16[32,1,32,2048]{3,2,1,0:T(8,128)(2,1)}), bf16[32,1,32,2048]{3,2,1,0:T(8,128)(2,1)}, u32[]{:S(2)}, u32[]{:S(2)}) async-start(bf16[32,1,32,2048]{3,2,1,0:T(8,128)(2,1)} %convert_bitcast_fusion), calls=%async_computation | async-start | bytes 8388608 | tf_op jit(solution)/shard_map/all_to_all | solution.py:107
  167.6 0.0 copy-start.2
  167.6 0.0 all-gather.9.cloned.1.call-start
  167.7 0.5 all-gather.9.cloned.1.call-update
  168.2 0.3 all-reduce.3.cloned.1.call-start
  168.5 0.1 copy.42
  168.6 0.2 reduce_window_sum.30
  168.8 0.1 copy.43
  168.8 0.0 copy-done.7
  168.8 0.1 copy.45
  168.9 0.1 reduce-window.7
  169.0 0.1 reduce.2
  169.1 0.1 convert_reduce_fusion
  169.2 0.0 copy-done.9
  169.2 0.1 select_reduce_fusion.1
  169.3 0.1 select_reduce_fusion
  169.5 0.0 reduce-scatter.2.cloned.1.call-done
  169.5 50.9 %all-to-all-done = bf16[32,1,32,2048]{3,2,1,0:T(8,128)(2,1)} async-done(((bf16[32,1,32,2048]{3,2,1,0:T(8,128)(2,1)}), bf16[32,1,32,2048]{3,2,1,0:T(8,128)(2,1)}, u32[]{:S(2)}, u32[]{:S(2)}) %all-to-all-start) | async-done | bytes 4194336 | tf_op jit(solution)/shard_map/all_to_all | solution.py:107
  220.4 4.3 %fusion.23 = f32[128,2048]{1,0:T(8,128)} fusion(f32[128,2048]{1,0:T(8,128)} %reduce-scatter.2.cloned.1.call-done, bf16[32,1,32,2048]{3,2,1,0:T(8,128)(2,1)} %all-to-all-done, s32[128,32]{0,1:T(8,128)S(1)} %copy.43, bf16[128,32]{0,1:T(8,128)(2,1)S(1)} %fusion.68), kind=kOutput, calls=%fused_computation.21 | convolution fusion | flops 537395200 | bytes 6316032 | tf_op jit(solution)/shard_map/kbt,btw->kw/dot_general | solution.py:114
  224.7 9.1 %all-gather.9.cloned.1.call-done = bf16[32,2048,16]{1,2,0:T(8,128)(2,1)} async-done(((bf16[8,2048,16]{1,2,0:T(8,128)(2,1)}), bf16[32,2048,16]{1,2,0:T(8,128)(2,1)}) %all-gather.9.cloned.1.call-update) | async-done | bytes 2097168 | tf_op jit(solution)/shard_map/all_gather | solution.py:128
  233.7 4.5 %fusion.26 = bf16[128,2048]{1,0:T(8,128)(2,1)S(1)} fusion(f32[128,2048]{1,0:T(8,128)} %fusion.23, bf16[32,16,2048]{2,0,1:T(8,128)(2,1)} %all-gather.11.cloned.1.call-done, bf16[32,16,2048]{2,1,0:T(8,128)(2,1)} %bitcast.110, bf16[128,2048]{1,0:T(8,128)(2,1)S(1)} %copy-done.2, pred[128,32]{0,1:T(8,128)(4,1)S(1)} %iota_compare_fusion.3), kind=kOutput, calls=%fused_computation.22 | convolution fusion | flops 537526272 | bytes 6295552 | tf_op jit(solution)/shard_map/dot_general | solution.py:44
  238.3 0.0 copy-start.3
  238.3 0.9 fusion.69
  239.2 0.0 all-reduce.3.cloned.1.call-update
  239.2 0.0 all-reduce.5.cloned.1.call-start
  239.3 100.2 %all-reduce.3.cloned.1.call-done = f32[24,2048]{1,0:T(8,128)} async-done(((f32[24,2048]{1,0:T(8,128)}), f32[24,2048]{1,0:T(8,128)}) %all-reduce.3.cloned.1.call-update) | async-done | bytes 196624 | tf_op jit(solution)/shard_map/psum | solution.py:138
  339.4 0.0 all-reduce.5.cloned.1.call-update
  339.4 42.3 %all-reduce.5.cloned.1.call-done = f32[24,2048]{1,0:T(8,128)} async-done(((f32[24,2048]{1,0:T(8,128)}), f32[24,2048]{1,0:T(8,128)}) %all-reduce.5.cloned.1.call-update) | async-done | bytes 196624 | tf_op jit(solution)/shard_map/psum | solution.py:138
  381.7 0.0 copy-done
  381.7 1.4 convolution_reduce_fusion
  383.2 9.8 %pmax.7 = f32[24,1]{0,1:T(1,128)} all-reduce(f32[24,1]{0,1:T(1,128)S(1)} %bitcast.112), channel_id=1, replica_groups=mesh['dp'=4,'tensor'=32] {'dp'}, use_global_device_ids=true, to_apply=%region_15.16 | all-reduce | flops 24 | bytes 192 | tf_op jit(solution)/shard_map/pmax | solution.py:143
  393.0 1.1 multiply_reduce_fusion
  394.1 0.5 sqrt.3
  394.6 0.0 copy-done.3
  (20 shorter events, 0.1 us)
Async XLA Ops:
  7.2 374.6 %copy-start = (bf16[2048,512]{1,0:T(8,128)(2,1)S(1)}, bf16[2048,512]{1,0:T(8,128)(2,1)}, u32[]{:S(2)}) copy-start(bf16[2048,512]{1,0:T(8,128)(2,1)} %param.31) | copy-start | bytes 6291460
  7.2 41.5 %copy-start.8 = (bf16[352,2048]{1,0:T(8,128)(2,1)S(1)}, bf16[352,2048]{1,0:T(8,128)(2,1)}, u32[]{:S(2)}) copy-start(bf16[352,2048]{1,0:T(8,128)(2,1)} %param.28) | copy-start | bytes 4325380
  7.2 37.7 %all-gather.7.cloned.1.call-start = ((), (), s32[]{:S(2)}) async-start(), calls=%async_computation.3 | async-start | bytes 2621440 | tf_op jit(solution)/shard_map/all_gather | solution.py:119
  11.5 109.0 %all-gather.5.cloned.1.call-start = ((), (), s32[]{:S(2)}) async-start(), calls=%async_computation.2 | async-start | bytes 17301504 | tf_op jit(solution)/shard_map/all_gather | solution.py:83
  12.2 157.3 %reduce-scatter.2.cloned.1.call-start = ((), (), s32[]{:S(2)}) async-start(), calls=%async_computation.4 | async-start | bytes 5242880 | tf_op jit(solution)/shard_map/reduce_scatter | solution.py:120
  55.0 1.0 copy-start.4
  55.0 2.1 copy-start.5
  55.0 169.6 %all-gather.11.cloned.1.call-start = ((), (), s32[]{:S(2)}) async-start(), calls=%async_computation.6 | async-start | bytes 2621440 | tf_op jit(solution)/shard_map/all_gather | solution.py:129
  128.5 2.1 copy-start.1
  162.3 6.5 %copy-start.7 = (s32[24]{0:T(128)S(1)}, s32[24]{0:T(128)}, u32[]{:S(2)}) copy-start(s32[24]{0:T(128)} %param.20) | copy-start | bytes 292
  162.3 6.9 %copy-start.9 = (s32[24]{0:T(128)S(1)}, s32[24]{0:T(128)}, u32[]{:S(2)}) copy-start(s32[24]{0:T(128)} %param.21) | copy-start | bytes 292
  162.3 7.0 %copy-start.10 = (s32[32]{0:T(128)S(1)}, s32[32]{0:T(128)}, u32[]{:S(2)}) copy-start(s32[32]{0:T(128)} %param.22) | copy-start | bytes 388
  162.4 7.1 %copy-start.6 = (bf16[128,6]{0,1:T(8,128)(2,1)S(1)}, bf16[128,6]{0,1:T(8,128)(2,1)}, u32[]{:S(2)}) copy-start(bf16[128,6]{0,1:T(8,128)(2,1)} %param.19) | copy-start | bytes 4612
  162.4 58.0 %all-to-all-start = ((bf16[32,1,32,2048]{3,2,1,0:T(8,128)(2,1)}), bf16[32,1,32,2048]{3,2,1,0:T(8,128)(2,1)}, u32[]{:S(2)}, u32[]{:S(2)}) async-start(bf16[32,1,32,2048]{3,2,1,0:T(8,128)(2,1)} %convert_bitcast_fusion), calls=%async_computation | async-start | bytes 8388608 | tf_op jit(solution)/shard_map/all_to_all | solution.py:107
  167.6 66.1 %copy-start.2 = (bf16[128,2048]{1,0:T(8,128)(2,1)S(1)}, bf16[128,2048]{1,0:T(8,128)(2,1)}, u32[]{:S(2)}) copy-start(bf16[128,2048]{1,0:T(8,128)(2,1)} %fusion.43) | copy-start | bytes 1572868
  167.6 66.1 %all-gather.9.cloned.1.call-start = ((), (), s32[]{:S(2)}) async-start(), calls=%async_computation.5 | async-start | bytes 2621440 | tf_op jit(solution)/shard_map/all_gather | solution.py:128
  168.2 171.2 %all-reduce.3.cloned.1.call-start = ((), (), s32[]{:S(2)}) async-start(), calls=%async_computation.7 | async-start | bytes 393216 | tf_op jit(solution)/shard_map/psum | solution.py:138
  238.3 156.3 %copy-start.3 = (bf16[128,2048]{1,0:T(8,128)(2,1)}, bf16[128,2048]{1,0:T(8,128)(2,1)S(1)}, u32[]{:S(2)}) copy-start(bf16[128,2048]{1,0:T(8,128)(2,1)S(1)} %fusion.26) | copy-start | bytes 1572868
  239.2 142.5 %all-reduce.5.cloned.1.call-start = ((), (), s32[]{:S(2)}) async-start(), calls=%async_computation.8 | async-start | bytes 393216 | tf_op jit(solution)/shard_map/psum | solution.py:138
Sparse Core Ops, SparseCore 0:
  11.6 33.2 all-gather.6
  47.7 72.6 all-gather.4
  122.8 46.1 reduce-scatter.1
  170.7 30.5 all-gather.10
  202.9 30.8 all-gather.8
  239.3 100.0 all-reduce.2
  341.7 39.9 all-reduce.4
